TPU v7x, 32 devices: a whole 2x2x4 slice. The times are simulated.
32 devices in a mesh: trainer: 16 (over z, x, core), store: 2 (over y).
Axes of the slice: x: 2, y: 2, z: 4, core: 2. Of those that a mesh axis runs over, the one named last changes fastest.
Arguments:
- memory: float32 [256, 512], P('store'), may hold values from -240 to 240
- event_feats: bfloat16 [25600, 128], P('store'), may hold values from -6 to 6
- batch_rows: int32 [16, 64], P('trainer', 'store'), may hold values from 0 to 127, as said below
- target_time: int32 [16, 64], P('trainer', 'store'), may hold values from 1024 to 2047
- neighbor_owner: int32 [16, 64, 100, 1], P('trainer', 'store'), may hold values from 0 to 1; in each aligned block of 3200 rows (0 to 3199, 3200 to 6399, ..., all dimensions but the last counted through in order) at most 3200 rows name the same one
- neighbor_event: int32 [16, 64, 100], P('trainer', 'store'), may hold values from 0 to 12799
- neighbor_time: int32 [16, 64, 100], P('trainer', 'store'), may hold values from 0 to 1023, as said below
- time_freq: float32 [128], replicated, may hold values from 0.001 to 1
- time_phase: float32 [128], replicated, may hold values from -3.140625 to 3.140625
- w_query: bfloat16 [512, 512], replicated, may hold values from -0.25 to 0.25
- w_key: bfloat16 [256, 512], replicated, may hold values from -0.375 to 0.375
- w_value: bfloat16 [256, 512], replicated, may hold values from -0.375 to 0.375
- ln_gain: float32 [512], replicated, may hold values from 0.5 to 1.5
- gru_input: bfloat16 [256, 1536], replicated, may hold values from -0.375 to 0.375
- gru_hidden: bfloat16 [512, 1536], replicated, may hold values from -0.25 to 0.25
- emb_cotangent: bfloat16 [16, 64, 512], P('trainer', 'store'), may hold values from -6 to 6
Outputs:
- embedding: bfloat16 [16, 64, 512], P('trainer', 'store')
- memory_next: float32 [16, 256, 512], P('trainer', 'store')
- key_value_grad: float32 [262144], P(('trainer', 'store'))
Inputs may be any that keep to these rules, and one draw needn't show every extreme that they name: `batch_rows`: the 32 entries that one device holds are distinct. `neighbor_owner`: among the 3200 neighbor rows of one device, no owner is named by more than 3200 rows. `neighbor_time`: along the 100 neighbors of a target, times never rise.
All inputs are finite; a program needn't handle non-finite values.
Results may differ from a plain program's by a relative error of at most 0.003.
The roundings to bfloat16 on the way count: a program that leaves them out, or rounds other values in their place, can miss the bound.
Values may be sent and summed in bfloat16 or wider, within the bound.
No kernel may reach another device: no remote copies, remote signals or barrier semaphores. Data moves between devices by JAX's collectives and lax.ppermute only.
A program may use at most 64 MiB of HBM per device.

v0:
```python
import math
import jax
import jax.numpy as jnp
from jax import lax
from jax.sharding import PartitionSpec as P

HEADS = 2
highest = lax.Precision.HIGHEST


def passed_along(value, axis, steps):
    count = lax.axis_size(axis)
    pairs = [(source, (source + steps) % count) for source in range(count)]
    return lax.ppermute(value, axis, pairs)


def key_inputs_of(feature_rows, target_times, neighbor_times, time_freq, time_phase):
    elapsed = (target_times[:, None] - neighbor_times).astype(jnp.float32)
    encoded = jnp.cos(elapsed[:, :, None] * time_freq + time_phase)
    return jnp.concatenate([feature_rows, encoded.astype(jnp.bfloat16)], axis=-1)


def memory_step(mem_rows, mem_low, latest_inputs, gru_input, gru_hidden):
    mem_width = mem_rows.shape[1]
    from_input = jnp.dot(latest_inputs, gru_input, preferred_element_type=jnp.float32)
    from_state = jnp.dot(mem_low, gru_hidden, preferred_element_type=jnp.float32)
    update_gate = jax.nn.sigmoid(from_input[:, :mem_width] + from_state[:, :mem_width])
    reset_gate = jax.nn.sigmoid(
        from_input[:, mem_width : 2 * mem_width] + from_state[:, mem_width : 2 * mem_width]
    )
    candidate = jnp.tanh(
        from_input[:, 2 * mem_width :] + reset_gate * from_state[:, 2 * mem_width :]
    )
    return (1.0 - update_gate) * candidate + update_gate * mem_rows


def attend_block(mem_rows, query, key_inputs, cotangent, w_key, w_value, ln_gain):
    block_size, neighbors, in_width = key_inputs.shape
    mem_width = w_key.shape[1]
    head_dim = mem_width // HEADS
    flat_inputs = key_inputs.reshape(block_size * neighbors, in_width)
    key_rows = jnp.dot(flat_inputs, w_key, preferred_element_type=jnp.float32).reshape(
        block_size, neighbors, HEADS, head_dim
    )
    value_rows = jnp.dot(flat_inputs, w_value, preferred_element_type=jnp.float32).reshape(
        block_size, neighbors, HEADS, head_dim
    )
    query_heads = query.reshape(block_size, HEADS, head_dim)
    score_scale = 1.0 / math.sqrt(head_dim)
    scores = jnp.einsum("bhd,bkhd->bhk", query_heads, key_rows, precision=highest) * score_scale
    row_max = jnp.max(scores, axis=-1, keepdims=True)
    exponent = jnp.exp(scores - row_max)
    attention = exponent / jnp.sum(exponent, axis=-1, keepdims=True)
    aggregate = jnp.einsum("bhk,bkhd->bhd", attention, value_rows, precision=highest).reshape(
        block_size, mem_width
    )
    summed = aggregate + mem_rows
    centered = summed - jnp.mean(summed, axis=-1, keepdims=True)
    inv_std = lax.rsqrt(jnp.mean(centered * centered, axis=-1, keepdims=True) + 1e-05)
    normed = centered * inv_std
    embedded = normed * ln_gain
    grad_normed = cotangent * ln_gain
    grad_summed = (
        grad_normed
        - jnp.mean(grad_normed, axis=-1, keepdims=True)
        - normed * jnp.mean(grad_normed * normed, axis=-1, keepdims=True)
    ) * inv_std
    grad_heads = grad_summed.reshape(block_size, HEADS, head_dim)
    grad_values = jnp.einsum("bhk,bhd->bkhd", attention, grad_heads, precision=highest)
    grad_attention = jnp.einsum("bhd,bkhd->bhk", grad_heads, value_rows, precision=highest)
    grad_scores = attention * (
        grad_attention - jnp.sum(attention * grad_attention, axis=-1, keepdims=True)
    )
    grad_keys = (
        jnp.einsum("bhk,bhd->bkhd", grad_scores, query_heads, precision=highest) * score_scale
    )
    contract = (((0,), (0,)), ((), ()))
    grad_key = lax.dot_general(
        flat_inputs,
        grad_keys.reshape(block_size * neighbors, mem_width).astype(jnp.bfloat16),
        contract,
        preferred_element_type=jnp.float32,
    )
    grad_value = lax.dot_general(
        flat_inputs,
        grad_values.reshape(block_size * neighbors, mem_width).astype(jnp.bfloat16),
        contract,
        preferred_element_type=jnp.float32,
    )
    return (embedded, jnp.stack([grad_key, grad_value]))


def on_device(
    memory,
    event_feats,
    batch_rows,
    target_time,
    neighbor_owner,
    neighbor_event,
    neighbor_time,
    time_freq,
    time_phase,
    w_query,
    w_key,
    w_value,
    ln_gain,
    gru_input,
    gru_hidden,
    emb_cotangent,
):
    targets = batch_rows.shape[1]
    neighbors = neighbor_event.shape[2]
    mem_width = memory.shape[1]
    held_rows = event_feats.shape[0]
    feat_width = event_feats.shape[1]
    total_rows = targets * neighbors
    owners = neighbor_owner.reshape(total_rows)
    local_ids = neighbor_event.reshape(total_rows)
    wanted = owners * held_rows + local_ids
    blank_rows = jnp.zeros((total_rows, feat_width), jnp.bfloat16)
    shard_rows = lax.all_gather(event_feats, "store", axis=0, tiled=True)
    offset = jnp.int32(0)
    shard_len = shard_rows.shape[0]
    inside = (wanted >= offset) & (wanted < offset + shard_len)
    position = jnp.clip(wanted, 0, shard_len - 1)
    feature_rows = jnp.where(inside[:, None], jnp.take(shard_rows, position, axis=0), blank_rows)
    target_rows = batch_rows[0]
    mem_rows = memory[target_rows]
    mem_low = mem_rows.astype(jnp.bfloat16)
    key_inputs = key_inputs_of(
        feature_rows.reshape(targets, neighbors, feat_width),
        target_time[0],
        neighbor_time[0],
        time_freq,
        time_phase,
    )
    new_rows = memory_step(mem_rows, mem_low, key_inputs[:, 0, :], gru_input, gru_hidden)
    memory_next = passed_along(memory.at[target_rows].set(new_rows), "trainer", 1)
    query = jnp.dot(mem_low, w_query, preferred_element_type=jnp.float32)
    replicas = lax.axis_size("trainer") * lax.axis_size("store")
    cotangent = emb_cotangent[0].astype(jnp.float32) * (1.0 / math.sqrt(replicas))
    block_size = math.gcd(targets, 8)
    blocks = targets // block_size

    def one_block(carried, inputs):
        rows_here, query_here, inputs_here, cot_here = inputs
        embedded, grads = attend_block(
            rows_here, query_here, inputs_here, cot_here, w_key, w_value, ln_gain
        )
        return (carried + grads, embedded)

    scanned = (
        mem_rows.reshape(blocks, block_size, mem_width),
        query.reshape(blocks, block_size, mem_width),
        key_inputs.reshape(blocks, block_size, neighbors, key_inputs.shape[2]),
        cotangent.reshape(blocks, block_size, mem_width),
    )
    zero_grads = jnp.zeros((2, w_key.shape[0], mem_width), jnp.float32)
    grads, embedded = lax.scan(one_block, zero_grads, scanned)
    embedding = embedded.reshape(targets, mem_width).astype(jnp.bfloat16)[None]
    flat_grad = grads.reshape(-1)
    summed_grad = lax.psum(flat_grad, ("trainer", "store"))
    share_len = flat_grad.shape[0] // replicas
    my_index = lax.axis_index("trainer") * lax.axis_size("store") + lax.axis_index("store")
    grad_share = lax.dynamic_slice_in_dim(summed_grad, my_index * share_len, share_len)
    return (embedding, memory_next[None], grad_share)


def solution(mesh):
    placed = (
        P("store", None),
        P("store", None),
        P("trainer", "store"),
        P("trainer", "store"),
        P("trainer", "store", None, None),
        P("trainer", "store", None),
        P("trainer", "store", None),
        P(),
        P(),
        P(),
        P(),
        P(),
        P(),
        P(),
        P(),
        P("trainer", "store", None),
    )
    return jax.shard_map(
        on_device,
        mesh=mesh,
        in_specs=placed,
        out_specs=(
            P("trainer", "store", None),
            P("trainer", "store", None),
            P(("trainer", "store")),
        ),
        check_vma=False,
    )
```

profile of v0, /device:TPU:0, one launch (start us, length us, event | category | flops | bytes accessed | tf_op | source)
XLA Modules:
  0.0 341.5 jit_solution(2309487747094358767)
XLA Ops:
  14.2 6.5 %cosine_convert_fusion.1 = bf16[4,8,100,128]{3,2,1,0:T(8,128)(2,1)} fusion(f32[128]{0:T(128)S(1)} %copy-done.24, f32[128]{0:T(128)S(1)} %copy-done.25, f32[4,8,100]{2,1,0:T(8,128)S(1)} %fusion.49), kind=kLoop, calls=%fused_computation.52 | loop fusion | flops 1228800 | bytes 833024 | tf_op jit(solution)/shard_map/convert_element_type | solution.py:20
  20.7 6.5 %cosine_convert_fusion = bf16[32,100,128]{2,1,0:T(8,128)(2,1)} fusion(f32[128]{0:T(128)S(1)} %copy-done.24, f32[128]{0:T(128)S(1)} %copy-done.25, f32[32,100]{1,0:T(8,128)S(1)} %fusion.48), kind=kLoop, calls=%fused_computation.51 | loop fusion | flops 1228800 | bytes 833024 | tf_op jit(solution)/shard_map/convert_element_type | solution.py:20
  28.3 67.3 %all-gather.2.cloned.1.call-done = bf16[25600,128]{1,0:T(8,128)(2,1)} async-done(((bf16[12800,128]{1,0:T(8,128)(2,1)}), bf16[25600,128]{1,0:T(8,128)(2,1)}) %all-gather.2.cloned.1.call-update) | async-done | bytes 6553616 | tf_op jit(solution)/shard_map/all_gather | solution.py:121
  95.6 9.5 %gather_fusion = bf16[3200,128]{1,0:T(8,128)(2,1)S(1)} fusion(bf16[25600,128]{1,0:T(8,128)(2,1)} %all-gather.2.cloned.1.call-done, s32[4096]{0:T(1024)S(1)} %pad_clamp_fusion), kind=kCustom, calls=%fused_computation | custom fusion | bytes 1651200 | tf_op jit(solution)/shard_map/jit(_take)/gather | solution.py:126
  108.9 89.1 %while.14 = (s32[]{:T(128)}, f32[2,256,512]{2,1,0:T(8,128)}, bf16[4,8,512]{2,1,0:T(8,128)(2,1)S(1)}, bf16[4,8,100,256]{3,2,1,0:T(8,128)(2,1)}, f32[4,8,512]{2,1,...) while((s32[]{:T(128)}, f32[2,256,512]{2,1,0:T(8,128)}, ...), condition=%wide.wide.region_8.9_spmd.clone, body=%wide.wide.region_0.8_spmd.clone.sunk | while | flops 856556288 | bytes 24278400 | solution.py:159
  111.0 1.6 fusion.134
  113.3 2.9 fusion.135
  125.7 1.6 convolution_bitcast_fusion.8
  132.3 1.6 fusion.134
  134.7 2.9 fusion.135
  141.4 1.5 fusion.142
  147.1 1.6 convolution_bitcast_fusion.8
  150.4 2.4 maximum_add_fusion.3
  154.9 1.6 fusion.134
  157.3 2.9 fusion.135
  169.7 1.6 convolution_bitcast_fusion.8
  173.0 2.4 maximum_add_fusion.3
  177.5 1.6 fusion.134
  179.8 2.9 fusion.135
  192.3 1.6 convolution_bitcast_fusion.8
  195.6 2.4 maximum_add_fusion.3
  198.7 2.5 copy.39
  204.6 9.2 %collective-permute-done = f32[128,512]{1,0:T(8,128)S(1)} collective-permute-done((f32[128,512]{1,0:T(8,128)S(1)}, f32[128,512]{1,0:T(8,128)S(1)}, u32[]{:S(2)}, u32[]{:S(2)}) %collective-permute-start) | collective-permute-done | bytes 262176 | tf_op jit(solution)/shard_map/ppermute | solution.py:14
  213.7 118.9 %all-reduce.2.cloned.1.call-done = f32[262144]{0:T(1024)} async-done(((f32[262144]{0:T(1024)}), f32[262144]{0:T(1024)}) %all-reduce.2.cloned.1.call-update) | async-done | bytes 1048592 | tf_op jit(solution)/shard_map/psum | solution.py:162
  (274 shorter events, 72.9 us)
Async XLA Ops:
  7.2 20.1 %copy-start = (bf16[512,1536]{1,0:T(8,128)(2,1)S(1)}, bf16[512,1536]{1,0:T(8,128)(2,1)}, u32[]{:S(2)}) copy-start(bf16[512,1536]{1,0:T(8,128)(2,1)} %param.32) | copy-start | bytes 4718596
  7.2 88.4 %all-gather.2.cloned.1.call-start = ((), (), s32[]{:S(2)}) async-start(), calls=%async_computation | async-start | bytes 9830400 | tf_op jit(solution)/shard_map/all_gather | solution.py:121
  8.3 2.9 copy-start.5
  8.3 3.6 %copy-start.12 = (bf16[512,512]{1,0:T(8,128)(2,1)S(1)}, bf16[512,512]{1,0:T(8,128)(2,1)}, u32[]{:S(2)}) copy-start(bf16[512,512]{1,0:T(8,128)(2,1)} %param.27) | copy-start | bytes 1572868
  8.4 4.4 %copy-start.20 = (s32[1,32,100]{2,1,0:T(8,128)S(1)}, s32[1,32,100]{2,1,0:T(8,128)}, u32[]{:S(2)}) copy-start(s32[1,32,100]{2,1,0:T(8,128)} %param.24) | copy-start | bytes 38404
  8.4 5.2 %copy-start.21 = (bf16[1,32,512]{2,1,0:T(8,128)(2,1)S(1)}, bf16[1,32,512]{2,1,0:T(8,128)(2,1)}, u32[]{:S(2)}) copy-start(bf16[1,32,512]{2,1,0:T(8,128)(2,1)} %param.33) | copy-start | bytes 98308
  8.4 5.8 %copy-start.24 = (f32[128]{0:T(128)S(1)}, f32[128]{0:T(128)}, u32[]{:S(2)}) copy-start(f32[128]{0:T(128)} %param.26) | copy-start | bytes 1540
  8.4 5.8 %copy-start.25 = (f32[128]{0:T(128)S(1)}, f32[128]{0:T(128)}, u32[]{:S(2)}) copy-start(f32[128]{0:T(128)} %param.25) | copy-start | bytes 1540
  8.4 324.2 %all-reduce.2.cloned.1.call-start = ((), (), s32[]{:S(2)}) async-start(), calls=%async_computation.1 | async-start | bytes 2097152 | tf_op jit(solution)/shard_map/psum | solution.py:162
  11.8 16.5 %copy-start.7 = (f32[32,512]{1,0:T(8,128)}, f32[32,512]{1,0:T(8,128)S(1)}, u32[]{:S(2)}) copy-start(f32[32,512]{1,0:T(8,128)S(1)} %gather_fusion.1) | copy-start | bytes 196612
  108.9 11.0 %copy-start.18 = (f32[2,256]{1,0:T(2,128)}, f32[2,256]{1,0:T(2,128)S(1)}, u32[]{:S(2)}) copy-start(f32[2,256]{1,0:T(2,128)S(1)} %get-tuple-element.306) | copy-start | bytes 6148 | tf_op jit(solution)/shard_map/while
  113.3 3.7 %copy-start.1 = (f32[1,8,512]{2,1,0:T(8,128)}, f32[1,8,512]{2,1,0:T(8,128)S(1)}, u32[]{:S(2)}) copy-start(f32[1,8,512]{2,1,0:T(8,128)S(1)} %get-tuple-element.263) | copy-start | bytes 49156 | tf_op jit(solution)/shard_map/while
  130.3 11.0 %copy-start.18 = (f32[2,256]{1,0:T(2,128)}, f32[2,256]{1,0:T(2,128)S(1)}, u32[]{:S(2)}) copy-start(f32[2,256]{1,0:T(2,128)S(1)} %get-tuple-element.306) | copy-start | bytes 6148 | tf_op jit(solution)/shard_map/while
  134.6 3.7 %copy-start.1 = (f32[1,8,512]{2,1,0:T(8,128)}, f32[1,8,512]{2,1,0:T(8,128)S(1)}, u32[]{:S(2)}) copy-start(f32[1,8,512]{2,1,0:T(8,128)S(1)} %get-tuple-element.263) | copy-start | bytes 49156 | tf_op jit(solution)/shard_map/while
  150.4 2.5 copy-start.15
  152.9 11.0 %copy-start.18 = (f32[2,256]{1,0:T(2,128)}, f32[2,256]{1,0:T(2,128)S(1)}, u32[]{:S(2)}) copy-start(f32[2,256]{1,0:T(2,128)S(1)} %get-tuple-element.306) | copy-start | bytes 6148 | tf_op jit(solution)/shard_map/while
  157.2 3.7 %copy-start.1 = (f32[1,8,512]{2,1,0:T(8,128)}, f32[1,8,512]{2,1,0:T(8,128)S(1)}, u32[]{:S(2)}) copy-start(f32[1,8,512]{2,1,0:T(8,128)S(1)} %get-tuple-element.263) | copy-start | bytes 49156 | tf_op jit(solution)/shard_map/while
  173.0 2.5 copy-start.15
  175.4 11.0 %copy-start.18 = (f32[2,256]{1,0:T(2,128)}, f32[2,256]{1,0:T(2,128)S(1)}, u32[]{:S(2)}) copy-start(f32[2,256]{1,0:T(2,128)S(1)} %get-tuple-element.306) | copy-start | bytes 6148 | tf_op jit(solution)/shard_map/while
  179.8 3.7 %copy-start.1 = (f32[1,8,512]{2,1,0:T(8,128)}, f32[1,8,512]{2,1,0:T(8,128)S(1)}, u32[]{:S(2)}) copy-start(f32[1,8,512]{2,1,0:T(8,128)S(1)} %get-tuple-element.263) | copy-start | bytes 49156 | tf_op jit(solution)/shard_map/while
  198.0 3.1 copy-start.2
  198.1 3.1 copy-start.22
  198.1 3.1 copy-start.23
  204.5 9.3 %collective-permute-start = (f32[128,512]{1,0:T(8,128)S(1)}, f32[128,512]{1,0:T(8,128)S(1)}, u32[]{:S(2)}, u32[]{:S(2)}) collective-permute-start(f32[128,512]{1,0:T(8,128)S(1)} %scatter_custom_fusion), channel_id=1, source_target_pairs={{0,2},{2,4},{4,6},{6,8},{8,10},{10,12},{12,14},{14,16},{16,18},{18... | collective-permute-start | bytes 786440 | tf_op jit(solution)/shard_map/ppermute | solution.py:14
  (33 other events, 47.0 us)
Sparse Core Ops, SparseCore 0:
  9.5 86.0 all-gather.1
  201.3 131.2 all-reduce.1
where the time goes:
time: 343 us; the launch traced here: 342 us
  waiting for transfers between devices  195 us (57%)
  other arithmetic  48.4 us (14%)
  local copies, waits for them, and re-layouts  42.7 us (12%)
  matrix products  39.7 us (12%)
  between operations  14.4 us (4%)
    psum x1, waiting for transfers between devices, on_device(): summed_grad = lax.psum(flat_grad, ('trainer', 'store'))  119 us
    all_gather x1, waiting for transfers between devices, on_device(): shard_rows = lax.all_gather(event_feats, 'store', axis=0, tiled=True)  67.3 us
    convert_element_type x2, other arithmetic, key_inputs_of(): encoded.astype(jnp.bfloat16)  13.1 us
    dot_general x4, matrix products, attend_block(): jnp.einsum('bhd,bkhd->bhk', query_heads, key_rows, precision=highest)  11.7 us
    gather x3, local copies, waits for them, and re-layouts, on_device(): jnp.take(shard_rows, position, axis=0)  10.7 us
    ppermute x1, waiting for transfers between devices, passed_along(): return lax.ppermute(value, axis, pairs)  9.18 us
    add x4, other arithmetic, one_block(): return (carried + grads, embedded)  8.43 us
    unnamed x57, local copies, waits for them, and re-layouts  7.36 us
  transfers between devices with their start and end apart: 3, of which 3 were waited for; matrix products, arithmetic and copies ran while one was open for 6% of the time, Pallas kernels for 0%

commit v1 on v0

--- a/solution.py
+++ b/solution.py
@@ -3,6 +3,7 @@
 import jax.numpy as jnp
 from jax import lax
 from jax.sharding import PartitionSpec as P
+from jax.lax import axis_index, ppermute
 
 HEADS = 2
 highest = lax.Precision.HIGHEST
@@ -108,6 +109,14 @@
     gru_hidden,
     emb_cotangent,
 ):
+
+    def divide_sheets_now(field_in, net_axis="store"):
+        return jnp.roll(
+            jnp.concatenate([field_in, ppermute(field_in, net_axis, [(0, 1), (1, 0)])], axis=0),
+            shift=axis_index(net_axis) * field_in.shape[0],
+            axis=0,
+        )
+
     targets = batch_rows.shape[1]
     neighbors = neighbor_event.shape[2]
     mem_width = memory.shape[1]
@@ -118,7 +127,7 @@
     local_ids = neighbor_event.reshape(total_rows)
     wanted = owners * held_rows + local_ids
     blank_rows = jnp.zeros((total_rows, feat_width), jnp.bfloat16)
-    shard_rows = lax.all_gather(event_feats, "store", axis=0, tiled=True)
+    shard_rows = divide_sheets_now(event_feats)
     offset = jnp.int32(0)
     shard_len = shard_rows.shape[0]
     inside = (wanted >= offset) & (wanted < offset + shard_len)

time: 343 us -> 365 us (1.064)
  other arithmetic: 48.4 us -> 81.4 us
  waiting for transfers between devices: 195 us -> 179 us
    all_gather x1 -> x0, waiting for transfers between devices: 67.3 us -> none  [on_device(): shard_rows = lax.all_gather(event_feats, 'store', axis=0, tiled=True)]
    ppermute x0 -> x1, waiting for transfers between devices: none -> 47.5 us  [divide_sheets_now(): ppermute(field_in, net_axis, [(0, 1), (1, 0)])]
    concatenate x0 -> x1, other arithmetic: none -> 30.9 us  [divide_sheets_now(): jnp.roll(jnp.concatenate([field_in, ppermute(field_in, net_axis, [(0, 1),...]
    unnamed x57 -> x55, local copies, waits for them, and re-layouts: 7.36 us -> 7.84 us
  transfers between devices with their start and end apart: 3 -> 3, of which waited for: 3 -> 3; matrix products, arithmetic and copies ran while one was open for 6% -> 7% of each run, Pallas kernels for 0% -> 0%
where the time goes in v1:
time: 365 us; the launch traced here: 363 us
  waiting for transfers between devices  179 us (49%)
  other arithmetic  81.4 us (22%)
  local copies, waits for them, and re-layouts  44.7 us (12%)
  matrix products  39.7 us (11%)
  between operations  14.4 us (4%)
    psum x1, waiting for transfers between devices, on_device(): summed_grad = lax.psum(flat_grad, ('trainer', 'store'))  122 us
    ppermute x1, waiting for transfers between devices, divide_sheets_now(): ppermute(field_in, net_axis, [(0, 1), (1, 0)])  47.5 us
    concatenate x1, other arithmetic, divide_sheets_now(): jnp.roll(jnp.concatenate([field_in, ppermute(field_in, net_axis, [(0, 1),...  30.9 us
    convert_element_type x2, other arithmetic, key_inputs_of(): encoded.astype(jnp.bfloat16)  13.1 us
    dot_general x4, matrix products, attend_block(): jnp.einsum('bhd,bkhd->bhk', query_heads, key_rows, precision=highest)  11.7 us
    gather x3, local copies, waits for them, and re-layouts, on_device(): jnp.take(shard_rows, position, axis=0)  10.8 us
    add x4, other arithmetic, one_block(): return (carried + grads, embedded)  8.6 us
    ppermute x1, waiting for transfers between devices, passed_along(): return lax.ppermute(value, axis, pairs)  8.57 us
  transfers between devices with their start and end apart: 3, of which 3 were waited for; matrix products, arithmetic and copies ran while one was open for 7% of the time, Pallas kernels for 0%

profile of v1, /device:TPU:0, one launch (start us, length us, event | category | flops | bytes accessed | tf_op | source)
XLA Modules:
  0.0 362.7 jit_solution(7352561628250748361)
XLA Ops:
  8.4 3.0 collective-permute-start
  21.0 6.6 %cosine_convert_fusion.1 = bf16[4,8,100,128]{3,2,1,0:T(8,128)(2,1)} fusion(f32[128]{0:T(128)S(1)} %copy-done.24, f32[128]{0:T(128)S(1)} %copy-done.25, f32[4,8,100]{2,1,0:T(8,128)S(1)} %fusion.52), kind=kLoop, calls=%fused_computation.59 | loop fusion | flops 1228800 | bytes 833024 | tf_op jit(solution)/shard_map/convert_element_type | solution.py:21
  27.5 6.5 %cosine_convert_fusion = bf16[32,100,128]{2,1,0:T(8,128)(2,1)} fusion(f32[128]{0:T(128)S(1)} %copy-done.24, f32[128]{0:T(128)S(1)} %copy-done.25, f32[32,100]{1,0:T(8,128)S(1)} %fusion.51), kind=kLoop, calls=%fused_computation.58 | loop fusion | flops 1228800 | bytes 833024 | tf_op jit(solution)/shard_map/convert_element_type | solution.py:21
  35.1 47.5 %collective-permute-done = bf16[12800,128]{1,0:T(8,128)(2,1)} collective-permute-done((bf16[12800,128]{1,0:T(8,128)(2,1)}, bf16[12800,128]{1,0:T(8,128)(2,1)}, u32[]{:S(2)}, u32[]{:S(2)}) %collective-permute-start) | collective-permute-done | bytes 3276832 | tf_op jit(solution)/shard_map/ppermute | solution.py:115
  82.6 30.9 %fusion.26 = bf16[25600,128]{1,0:T(8,128)(2,1)} fusion(s32[]{:T(128)S(6)} %select_n.65, bf16[12800,128]{1,0:T(8,128)(2,1)S(1)} %copy-done.5, bf16[12800,128]{1,0:T(8,128)(2,1)} %collective-permute-done), kind=kLoop, calls=%fused_computation.56 | loop fusion | flops 26214400 | bytes 13107204 | tf_op jit(solution)/shard_map/jit(_roll_dynamic)/concatenate | solution.py:114
  113.5 9.6 %gather_fusion = bf16[3200,128]{1,0:T(8,128)(2,1)S(1)} fusion(bf16[25600,128]{1,0:T(8,128)(2,1)} %fusion.26, s32[4096]{0:T(1024)S(1)} %pad_clamp_fusion), kind=kCustom, calls=%fused_computation | custom fusion | bytes 1651200 | tf_op jit(solution)/shard_map/jit(_take)/gather | solution.py:135
  127.0 89.3 %while.14 = (s32[]{:T(128)}, f32[2,256,512]{2,1,0:T(8,128)}, bf16[4,8,512]{2,1,0:T(8,128)(2,1)S(1)}, bf16[4,8,100,256]{3,2,1,0:T(8,128)(2,1)}, f32[4,8,512]{2,1,...) while((s32[]{:T(128)}, f32[2,256,512]{2,1,0:T(8,128)}, ...), condition=%wide.wide.region_8.9_spmd.clone, body=%wide.wide.region_0.8_spmd.clone.sunk | while | flops 856556288 | bytes 24278400 | solution.py:168
  129.1 1.6 fusion.137
  131.4 2.9 fusion.138
  143.8 1.6 convolution_bitcast_fusion.8
  150.5 1.6 fusion.137
  152.8 2.9 fusion.138
  165.2 1.6 convolution_bitcast_fusion.8
  168.6 2.5 maximum_add_fusion.3
  173.1 1.6 fusion.137
  175.5 2.9 fusion.138
  187.9 1.6 convolution_bitcast_fusion.8
  191.2 2.5 maximum_add_fusion.3
  198.1 2.9 fusion.138
  210.5 1.6 convolution_bitcast_fusion.8
  213.8 2.5 maximum_add_fusion.3
  216.9 2.5 copy.39
  222.8 8.6 %collective-permute-done.1 = f32[128,512]{1,0:T(8,128)S(1)} collective-permute-done((f32[128,512]{1,0:T(8,128)S(1)}, f32[128,512]{1,0:T(8,128)S(1)}, u32[]{:S(2)}, u32[]{:S(2)}) %collective-permute-start.1) | collective-permute-done | bytes 262176 | tf_op jit(solution)/shard_map/ppermute | solution.py:15
  231.4 122.4 %all-reduce.2.cloned.1.call-done = f32[262144]{0:T(1024)} async-done(((f32[262144]{0:T(1024)}), f32[262144]{0:T(1024)}) %all-reduce.2.cloned.1.call-update) | async-done | bytes 1048592 | tf_op jit(solution)/shard_map/psum | solution.py:171
  (272 shorter events, 79.8 us)
Async XLA Ops:
  7.2 26.9 %copy-start = (bf16[512,1536]{1,0:T(8,128)(2,1)S(1)}, bf16[512,1536]{1,0:T(8,128)(2,1)}, u32[]{:S(2)}) copy-start(bf16[512,1536]{1,0:T(8,128)(2,1)} %param.32) | copy-start | bytes 4718596
  7.2 12.3 %copy-start.26 = (s32[1,32]{1,0:T(1,128)S(1)}, s32[1,32]{1,0:T(1,128)}, u32[]{:S(2)}) copy-start(s32[1,32]{1,0:T(1,128)} %param.21) | copy-start | bytes 388
  7.2 12.5 %copy-start.17 = (s32[1,32,100,1]{2,3,1,0:T(1,128)S(1)}, s32[1,32,100,1]{2,3,1,0:T(1,128)}, u32[]{:S(2)}) copy-start(s32[1,32,100,1]{2,3,1,0:T(1,128)} %param.22) | copy-start | bytes 38404
  7.2 12.5 %copy-start.16 = (s32[1,32,100]{2,1,0:T(8,128)S(1)}, s32[1,32,100]{2,1,0:T(8,128)}, u32[]{:S(2)}) copy-start(s32[1,32,100]{2,1,0:T(8,128)} %param.23) | copy-start | bytes 38404
  7.2 12.3 %copy-start.20 = (s32[1,32,100]{2,1,0:T(8,128)S(1)}, s32[1,32,100]{2,1,0:T(8,128)}, u32[]{:S(2)}) copy-start(s32[1,32,100]{2,1,0:T(8,128)} %param.24) | copy-start | bytes 38404
  7.2 13.7 %copy-start.25 = (f32[128]{0:T(128)S(1)}, f32[128]{0:T(128)}, u32[]{:S(2)}) copy-start(f32[128]{0:T(128)} %param.25) | copy-start | bytes 1540
  7.2 13.7 %copy-start.24 = (f32[128]{0:T(128)S(1)}, f32[128]{0:T(128)}, u32[]{:S(2)}) copy-start(f32[128]{0:T(128)} %param.26) | copy-start | bytes 1540
  7.2 11.4 %copy-start.13 = (bf16[512,512]{1,0:T(8,128)(2,1)S(1)}, bf16[512,512]{1,0:T(8,128)(2,1)}, u32[]{:S(2)}) copy-start(bf16[512,512]{1,0:T(8,128)(2,1)} %param.27) | copy-start | bytes 1572868
  7.3 13.1 %copy-start.21 = (bf16[1,32,512]{2,1,0:T(8,128)(2,1)S(1)}, bf16[1,32,512]{2,1,0:T(8,128)(2,1)}, u32[]{:S(2)}) copy-start(bf16[1,32,512]{2,1,0:T(8,128)(2,1)} %param.33) | copy-start | bytes 98308
  7.3 346.5 %all-reduce.2.cloned.1.call-start = ((), (), s32[]{:S(2)}) async-start(), calls=%async_computation | async-start | bytes 2097152 | tf_op jit(solution)/shard_map/psum | solution.py:171
  8.4 25.6 %copy-start.6 = (f32[128,512]{1,0:T(8,128)}, f32[128,512]{1,0:T(8,128)S(1)}, u32[]{:S(2)}) copy-start(f32[128,512]{1,0:T(8,128)S(1)} %copy.105) | copy-start | bytes 786436
  8.4 74.2 %collective-permute-start = (bf16[12800,128]{1,0:T(8,128)(2,1)}, bf16[12800,128]{1,0:T(8,128)(2,1)}, u32[]{:S(2)}, u32[]{:S(2)}) collective-permute-start(bf16[12800,128]{1,0:T(8,128)(2,1)} %param.19), channel_id=1, source_target_pairs={{0,1},{1,0},{2,3},{3,2},{4,5},{5,4},{6,7},{7,6},{8,9},{9,8},{10,11... | collective-permute-start | bytes 9830408 | tf_op jit(solution)/shard_map/ppermute | solution.py:115
  18.6 16.5 %copy-start.8 = (f32[32,512]{1,0:T(8,128)}, f32[32,512]{1,0:T(8,128)S(1)}, u32[]{:S(2)}) copy-start(f32[32,512]{1,0:T(8,128)S(1)} %gather_fusion.1) | copy-start | bytes 196612
  20.9 61.7 %copy-start.5 = (bf16[12800,128]{1,0:T(8,128)(2,1)S(1)}, bf16[12800,128]{1,0:T(8,128)(2,1)}, u32[]{:S(2)}) copy-start(bf16[12800,128]{1,0:T(8,128)(2,1)} %param.19) | copy-start | bytes 9830404
  127.0 11.0 %copy-start.18 = (f32[2,256]{1,0:T(2,128)}, f32[2,256]{1,0:T(2,128)S(1)}, u32[]{:S(2)}) copy-start(f32[2,256]{1,0:T(2,128)S(1)} %get-tuple-element.306) | copy-start | bytes 6148 | tf_op jit(solution)/shard_map/while
  131.4 3.7 %copy-start.1 = (f32[1,8,512]{2,1,0:T(8,128)}, f32[1,8,512]{2,1,0:T(8,128)S(1)}, u32[]{:S(2)}) copy-start(f32[1,8,512]{2,1,0:T(8,128)S(1)} %get-tuple-element.263) | copy-start | bytes 49156 | tf_op jit(solution)/shard_map/while
  148.4 11.1 %copy-start.18 = (f32[2,256]{1,0:T(2,128)}, f32[2,256]{1,0:T(2,128)S(1)}, u32[]{:S(2)}) copy-start(f32[2,256]{1,0:T(2,128)S(1)} %get-tuple-element.306) | copy-start | bytes 6148 | tf_op jit(solution)/shard_map/while
  152.8 3.7 %copy-start.1 = (f32[1,8,512]{2,1,0:T(8,128)}, f32[1,8,512]{2,1,0:T(8,128)S(1)}, u32[]{:S(2)}) copy-start(f32[1,8,512]{2,1,0:T(8,128)S(1)} %get-tuple-element.263) | copy-start | bytes 49156 | tf_op jit(solution)/shard_map/while
  171.0 11.1 %copy-start.18 = (f32[2,256]{1,0:T(2,128)}, f32[2,256]{1,0:T(2,128)S(1)}, u32[]{:S(2)}) copy-start(f32[2,256]{1,0:T(2,128)S(1)} %get-tuple-element.306) | copy-start | bytes 6148 | tf_op jit(solution)/shard_map/while
  175.4 3.7 %copy-start.1 = (f32[1,8,512]{2,1,0:T(8,128)}, f32[1,8,512]{2,1,0:T(8,128)S(1)}, u32[]{:S(2)}) copy-start(f32[1,8,512]{2,1,0:T(8,128)S(1)} %get-tuple-element.263) | copy-start | bytes 49156 | tf_op jit(solution)/shard_map/while
  193.7 11.1 %copy-start.18 = (f32[2,256]{1,0:T(2,128)}, f32[2,256]{1,0:T(2,128)S(1)}, u32[]{:S(2)}) copy-start(f32[2,256]{1,0:T(2,128)S(1)} %get-tuple-element.306) | copy-start | bytes 6148 | tf_op jit(solution)/shard_map/while
  198.1 3.7 %copy-start.1 = (f32[1,8,512]{2,1,0:T(8,128)}, f32[1,8,512]{2,1,0:T(8,128)S(1)}, u32[]{:S(2)}) copy-start(f32[1,8,512]{2,1,0:T(8,128)S(1)} %get-tuple-element.263) | copy-start | bytes 49156 | tf_op jit(solution)/shard_map/while
  216.3 3.1 copy-start.2
  222.7 8.6 %collective-permute-start.1 = (f32[128,512]{1,0:T(8,128)S(1)}, f32[128,512]{1,0:T(8,128)S(1)}, u32[]{:S(2)}, u32[]{:S(2)}) collective-permute-start(f32[128,512]{1,0:T(8,128)S(1)} %scatter_custom_fusion), channel_id=1, source_target_pairs={{0,2},{2,4},{4,6},{6,8},{8,10},{10,12},{12,14},{14,16},{16,18},{18... | collective-permute-start | bytes 786440 | tf_op jit(solution)/shard_map/ppermute | solution.py:15
  (32 other events, 50.2 us)
Sparse Core Ops, SparseCore 0:
  219.5 134.2 all-reduce.1
